TPU v7x, 256 devices: a whole 4x4x8 slice. The times are simulated.
256 devices in a mesh: sec: 16 (over z, core), term: 16 (over y, x).
Axes of the slice: x: 4, y: 4, z: 8, core: 2. Of those that a mesh axis runs over, the one named last changes fastest.
Arguments:
- psi: bfloat16 [16, 512, 512], P('sec'), may hold values from -6 to 6
- left_ops: bfloat16 [16, 96, 512, 512], P('sec', 'term'), may hold values from -0.078125 to 0.078125
- right_ops: bfloat16 [16, 96, 512, 512], P('sec', 'term'), may hold values from -0.078125 to 0.078125
- term_mask: int32 [16, 96], P('sec', 'term'), may hold values 0 or 1
- pair_src: int32 [16], P('sec'), may hold values from 0 to 15, each once
- pair_dst: int32 [16], P('sec'), may hold values from 0 to 15, each once
Outputs:
- sigma: bfloat16 [16, 512, 512], P('sec')
Inputs may be any that keep to these rules, and one draw needn't show every extreme that they name: `pair_src`: each of the 16 sector blocks is the source of exactly one pair. `pair_dst`: each of the 16 sector blocks is the target of exactly one pair.
All inputs are finite; a program needn't handle non-finite values. No bound on the sum of `term_mask` on one device may be relied on, other than what follows from the above.
Results may differ from a plain program's by a relative error of at most 0.0065.
Values may be sent and summed in bfloat16 or wider, within the bound.
A program may use at most 64 MiB of HBM per device.

v0:
```python
import jax
import jax.numpy as jnp
from jax import lax
from jax.sharding import PartitionSpec as P


def in_blocks(value, dim, peers):
    shape = value.shape
    pieces = value.reshape(*shape[:dim], peers, shape[dim] // peers, *shape[dim + 1 :])
    return jnp.moveaxis(pieces, dim, 0)


def sent_and_summed(value, axis, dim):
    pieces = in_blocks(value, dim, lax.axis_size(axis))
    arrived = lax.all_to_all(pieces, axis, split_axis=0, concat_axis=0, tiled=True)
    return arrived.astype(jnp.float32).sum(axis=0)


def in_one_piece(arrays, axis, dim, along):
    columns = [a.reshape(*a.shape[:along], -1) for a in arrays]
    both = jnp.concatenate(columns, axis=along)
    filled, at, finished = (lax.all_gather(both, axis, axis=dim, tiled=True), 0, [])
    for a, column in zip(arrays, columns):
        piece = filled[..., at : at + column.shape[along]]
        finished.append(piece.reshape(*piece.shape[:along], *a.shape[along:]))
        at += column.shape[along]
    return tuple(finished)


def in_order(pieces, dim):
    pieces = jnp.moveaxis(pieces, 0, dim)
    shape = pieces.shape
    return pieces.reshape(*shape[:dim], shape[dim] * shape[dim + 1], *shape[dim + 2 :])


def copy_for_each(value, axis):
    peers = lax.axis_size(axis)
    return lax.all_to_all(
        jnp.broadcast_to(value[None], (peers, *value.shape)), axis, 0, 0, tiled=True
    )


def gathered_copies(value, axis, dim):
    return in_order(copy_for_each(value, axis), dim)


def local(psi, left_ops, right_ops, term_mask, pair_src, pair_dst):
    whole = lax.all_gather(psi, "sec", axis=0, tiled=True)
    order = psi.shape[1]
    local_pairs = psi.shape[0]
    local_terms = left_ops.shape[1]
    zero_block = jnp.zeros((order, order), jnp.float32)
    source = pair_src[0]
    target = pair_dst[0]
    src_block = lax.dynamic_index_in_dim(whole, source, 0, keepdims=False)
    dst_block = lax.dynamic_index_in_dim(whole, target, 0, keepdims=False)

    def term_step(acc, term):

        def active(carry):
            fwd_acc, adj_acc = carry
            left = left_ops[0, term]
            right = right_ops[0, term]
            inner_fwd = jnp.dot(left, src_block, preferred_element_type=jnp.float32).astype(
                jnp.bfloat16
            )
            inner_adj = jnp.dot(left.T, dst_block, preferred_element_type=jnp.float32).astype(
                jnp.bfloat16
            )
            fwd_acc = fwd_acc + jnp.dot(inner_fwd, right.T, preferred_element_type=jnp.float32)
            adj_acc = adj_acc + jnp.dot(inner_adj, right, preferred_element_type=jnp.float32)
            return (fwd_acc, adj_acc)

        return (lax.cond(term_mask[0, term] == 1, active, lambda carry: carry, acc), None)

    (fwd, adj), _ = lax.scan(
        term_step, (zero_block, zero_block), jnp.arange(local_terms, dtype=jnp.int32)
    )
    fwd_list = [fwd]
    adj_list = [adj]
    stacked = jnp.stack([jnp.stack(fwd_list), jnp.stack(adj_list)], axis=1)
    pieces = sent_and_summed(stacked.astype(jnp.bfloat16), "term", 2)
    all_pieces, all_src, all_dst = in_one_piece(
        (pieces, pair_src.astype(jnp.float32), pair_dst.astype(jnp.float32)), "sec", 0, 1
    )
    mine = (lax.axis_index("sec") * local_pairs + jnp.arange(local_pairs, dtype=jnp.int32)).astype(
        jnp.float32
    )
    pick_fwd = (all_dst[None, :] == mine[:, None]).astype(jnp.float32)
    pick_adj = (all_src[None, :] == mine[:, None]).astype(jnp.float32)
    rows_fwd = jnp.einsum(
        "sk,krc->src", pick_fwd, all_pieces[:, 0], precision=lax.Precision.HIGHEST
    )
    rows_adj = jnp.einsum(
        "sk,krc->src", pick_adj, all_pieces[:, 1], precision=lax.Precision.HIGHEST
    )
    rows = (rows_fwd + rows_adj).astype(jnp.bfloat16)
    return gathered_copies(rows, "term", 1)


def solution(mesh):
    placed = (
        P("sec", None, None),
        P("sec", "term", None, None),
        P("sec", "term", None, None),
        P("sec", "term"),
        P("sec"),
        P("sec"),
    )
    return jax.shard_map(
        local, mesh=mesh, in_specs=placed, out_specs=P("sec", None, None), check_vma=False
    )
```

profile of v0, /device:TPU:1, one launch (start us, length us, event | category | flops | bytes accessed | tf_op | source)
XLA Modules:
  0.0 217.1 jit_solution(3146875595708951832)
XLA Ops:
  6.5 0.0 copy-start.1
  6.5 0.0 all-gather.4.cloned.1.call-start
  6.5 0.7 all-gather.4.cloned.1.call-update
  8.6 60.7 %all-gather.4.cloned.1.call-done = bf16[16,512,512]{2,1,0:T(8,128)(2,1)} async-done(((bf16[1,512,512]{2,1,0:T(8,128)(2,1)}), bf16[16,512,512]{2,1,0:T(8,128)(2,1)}) %all-gather.4.cloned.1.call-update) | async-done | bytes 8388624 | tf_op jit(solution)/shard_map/all_gather | solution.py:48
  69.2 1.3 dynamic-slice_bitcast_fusion
  70.5 0.1 broadcast_in_dim.4
  70.6 0.1 broadcast_in_dim.4.clone
  70.8 0.0 copy-done.1
  70.8 53.7 %while.12 = (s32[]{:T(128)}, f32[512,512]{1,0:T(8,128)S(1)}, f32[512,512]{1,0:T(8,128)S(1)}, s32[6]{0:T(128)S(1)}, s32[1,6]{1,0:T(1,128)S(1)}, /*index=5*/bf16[1...) while((s32[]{:T(128)}, f32[512,512]{1,0:T(8,128)S(1)}, ...), condition=%wide.region_3.4_spmd, body=%wide.region_0.3_spmd.sunk | while | flops 1074790400 | bytes 7342387 | solution.py:76
  70.8 0.7 dynamic_slice.44
  73.5 0.6 fusion.29
  74.7 6.0 %conditional.2 = ((f32[512,512]{1,0:T(8,128)S(1)}, f32[512,512]{1,0:T(8,128)S(1)})) conditional(s32[]{:T(128)} %bitcast.55, (f32[512,512]{1,0:T(8,128)S(1)}, f32[512,512]{1,0:T(8,128)S(1)}) %tuple.30, (s32[]{:T(128)}, bf16[1,6,512,512]{3,2,1,0:T(8,128)(2,1)}, bf16[512,512]{1,0:T(8,128)(2,1)S(1)}, bf16[1,6,512,512]{3,2,1,0:T(8,128)(2,1)}, ...), branch_computations={%region_1.1_spmd, %region_2.2_spmd} | conditional | flops 1074790400 | bytes 7342138 | solution.py:74
  76.8 1.9 convolution_add_fusion
  78.8 1.9 convolution_add_fusion.1
  80.7 0.7 dynamic_slice.44
  83.4 0.6 fusion.29
  84.7 6.0 %conditional.2 = ((f32[512,512]{1,0:T(8,128)S(1)}, f32[512,512]{1,0:T(8,128)S(1)})) conditional(s32[]{:T(128)} %bitcast.55, (f32[512,512]{1,0:T(8,128)S(1)}, f32[512,512]{1,0:T(8,128)S(1)}) %tuple.30, (s32[]{:T(128)}, bf16[1,6,512,512]{3,2,1,0:T(8,128)(2,1)}, bf16[512,512]{1,0:T(8,128)(2,1)S(1)}, bf16[1,6,512,512]{3,2,1,0:T(8,128)(2,1)}, ...), branch_computations={%region_1.1_spmd, %region_2.2_spmd} | conditional | flops 1074790400 | bytes 7342138 | solution.py:74
  86.7 1.9 convolution_add_fusion
  88.7 1.9 convolution_add_fusion.1
  90.7 0.7 dynamic_slice.44
  93.4 0.6 fusion.29
  94.6 6.0 %conditional.2 = ((f32[512,512]{1,0:T(8,128)S(1)}, f32[512,512]{1,0:T(8,128)S(1)})) conditional(s32[]{:T(128)} %bitcast.55, (f32[512,512]{1,0:T(8,128)S(1)}, f32[512,512]{1,0:T(8,128)S(1)}) %tuple.30, (s32[]{:T(128)}, bf16[1,6,512,512]{3,2,1,0:T(8,128)(2,1)}, bf16[512,512]{1,0:T(8,128)(2,1)S(1)}, bf16[1,6,512,512]{3,2,1,0:T(8,128)(2,1)}, ...), branch_computations={%region_1.1_spmd, %region_2.2_spmd} | conditional | flops 1074790400 | bytes 7342138 | solution.py:74
  96.7 2.0 convolution_add_fusion
  98.6 1.9 convolution_add_fusion.1
  100.6 0.7 dynamic_slice.44
  103.3 0.6 fusion.29
  104.6 0.7 dynamic_slice.44
  107.3 0.6 fusion.29
  108.6 6.0 %conditional.2 = ((f32[512,512]{1,0:T(8,128)S(1)}, f32[512,512]{1,0:T(8,128)S(1)})) conditional(s32[]{:T(128)} %bitcast.55, (f32[512,512]{1,0:T(8,128)S(1)}, f32[512,512]{1,0:T(8,128)S(1)}) %tuple.30, (s32[]{:T(128)}, bf16[1,6,512,512]{3,2,1,0:T(8,128)(2,1)}, bf16[512,512]{1,0:T(8,128)(2,1)S(1)}, bf16[1,6,512,512]{3,2,1,0:T(8,128)(2,1)}, ...), branch_computations={%region_1.1_spmd, %region_2.2_spmd} | conditional | flops 1074790400 | bytes 7342138 | solution.py:74
  110.6 1.9 convolution_add_fusion
  112.6 1.9 convolution_add_fusion.1
  114.5 0.7 dynamic_slice.44
  117.2 0.6 fusion.29
  118.5 6.0 %conditional.2 = ((f32[512,512]{1,0:T(8,128)S(1)}, f32[512,512]{1,0:T(8,128)S(1)})) conditional(s32[]{:T(128)} %bitcast.55, (f32[512,512]{1,0:T(8,128)S(1)}, f32[512,512]{1,0:T(8,128)S(1)}) %tuple.30, (s32[]{:T(128)}, bf16[1,6,512,512]{3,2,1,0:T(8,128)(2,1)}, bf16[512,512]{1,0:T(8,128)(2,1)S(1)}, bf16[1,6,512,512]{3,2,1,0:T(8,128)(2,1)}, ...), branch_computations={%region_1.1_spmd, %region_2.2_spmd} | conditional | flops 1074790400 | bytes 7342138 | solution.py:74
  120.6 1.9 convolution_add_fusion
  122.5 1.9 convolution_add_fusion.1
  124.5 0.1 convert.9
  124.6 0.1 convert.10
  124.6 1.1 maximum_bitcast_fusion
  125.7 6.3 %all-to-all-start = ((bf16[16,1,2,32,512]{4,3,2,1,0:T(8,128)(2,1)}), bf16[16,1,2,32,512]{4,3,2,1,0:T(8,128)(2,1)S(1)}, u32[]{:S(2)}, u32[]{:S(2)}) async-start(bf16[16,1,2,32,512]{4,3,2,1,0:T(8,128)(2,1)} %maximum_bitcast_fusion), calls=%async_computation | async-start | bytes 2097152 | tf_op jit(solution)/shard_map/all_to_all | solution.py:15
  132.0 0.0 all-gather.6.cloned.1.call-start
  132.0 16.1 %all-to-all-done = bf16[16,1,2,32,512]{4,3,2,1,0:T(8,128)(2,1)S(1)} async-done(((bf16[16,1,2,32,512]{4,3,2,1,0:T(8,128)(2,1)}), bf16[16,1,2,32,512]{4,3,2,1,0:T(8,128)(2,1)S(1)}, u32[]{:S(2)}, u32[]{:S(2)}) %all-to-all-start) | async-done | bytes 1048608 | tf_op jit(solution)/shard_map/all_to_all | solution.py:15
  148.1 0.1 convert_reduce_fusion
  148.3 0.1 reshape.86
  148.5 0.1 dynamic-update-slice.2
  148.6 0.0 copy-start
  148.6 0.7 copy-done
  149.3 0.0 all-gather.6.cloned.1.call-update
  149.3 37.2 %all-gather.6.cloned.1.call-done = f32[16,1,32770]{2,1,0:T(1,128)} async-done(((f32[1,1,32770]{2,1,0:T(1,128)}), f32[16,1,32770]{2,1,0:T(1,128)}) %all-gather.6.cloned.1.call-update) | async-done | bytes 2097296 | tf_op jit(solution)/shard_map/all_gather | solution.py:22
  186.5 1.7 copy.20
  188.2 0.1 slice.21
  188.4 1.2 copy.12
  189.6 0.3 slice_bitcast_fusion.1
  189.9 0.2 fusion.21
  190.1 1.1 fusion.18
  191.2 1.1 fusion.16
  192.3 17.1 %all_to_all.10 = bf16[16,1,32,512]{3,2,1,0:T(8,128)(2,1)S(1)} all-to-all(bf16[16,1,32,512]{3,2,1,0:T(8,128)(2,1)S(1)} %broadcast_in_dim.5), channel_id=1, replica_groups=mesh['sec'=16,'term'=16] {'term'}, dimensions={0} | all-to-all | bytes 1048576 | tf_op jit(solution)/shard_map/all_to_all | solution.py:38
  209.5 0.8 copy.39
  (6 shorter events, 0.1 us)
Async XLA Ops:
  6.5 64.2 %copy-start.1 = (s32[1,6]{1,0:T(1,128)S(1)}, s32[1,6]{1,0:T(1,128)}, u32[]{:S(2)}) copy-start(s32[1,6]{1,0:T(1,128)} %param.13) | copy-start | bytes 76
  6.5 62.7 %all-gather.4.cloned.1.call-start = ((), (), s32[]{:S(2)}) async-start(), calls=%async_computation.2 | async-start | bytes 8912896 | tf_op jit(solution)/shard_map/all_gather | solution.py:48
  125.7 22.4 %all-to-all-start = ((bf16[16,1,2,32,512]{4,3,2,1,0:T(8,128)(2,1)}), bf16[16,1,2,32,512]{4,3,2,1,0:T(8,128)(2,1)S(1)}, u32[]{:S(2)}, u32[]{:S(2)}) async-start(bf16[16,1,2,32,512]{4,3,2,1,0:T(8,128)(2,1)} %maximum_bitcast_fusion), calls=%async_computation | async-start | bytes 2097152 | tf_op jit(solution)/shard_map/all_to_all | solution.py:15
  132.0 54.5 %all-gather.6.cloned.1.call-start = ((), (), s32[]{:S(2)}) async-start(), calls=%async_computation.3 | async-start | bytes 2236928 | tf_op jit(solution)/shard_map/all_gather | solution.py:22
  148.6 0.7 copy-start
Sparse Core Ops, SparseCore 0:
  9.2 60.0 all-gather.3
  149.4 37.0 all-gather.5
where the time goes:
time: 218 us; the launch traced here: 217 us
  waiting for transfers between devices  115 us (53%)
  loops' own time  26.7 us (12%)
  matrix products  21.6 us (10%)
  blocking collectives  17.1 us (8%)
  between operations  14.9 us (7%)
  local copies, waits for them, and re-layouts  10.6 us (5%)
  starting transfers between devices  6.3 us (3%)
  other arithmetic  5.21 us (2%)
    all_gather x1, waiting for transfers between devices, local(): whole = lax.all_gather(psi, 'sec', axis=0, tiled=True)  60.7 us
    all_gather x1, waiting for transfers between devices, in_one_piece(): lax.all_gather(both, axis, axis=dim, tiled=True)  37.2 us
    all_to_all x1, blocking collectives, copy_for_each(): lax.all_to_all(jnp.broadcast_to(value[None], (peers, *value.shape)), axis...  17.1 us
    another operation x1, loops' own time, local(): lax.scan(term_step, (zero_block, zero_block), jnp.arange(local_terms, dty...  16.3 us
    all_to_all x1, waiting for transfers between devices, sent_and_summed(): lax.all_to_all(pieces, axis, split_axis=0, concat_axis=0, tiled=True)  16.1 us
    another operation x6, loops' own time, term_step(): lax.cond(term_mask[0, term] == 1, active, lambda carry: carry, acc)  10.4 us
    dot_general x5, matrix products, active(): jnp.dot(inner_adj, right, preferred_element_type=jnp.float32)  9.73 us
    dot_general x5, matrix products, active(): jnp.dot(inner_fwd, right.T, preferred_element_type=jnp.float32)  9.7 us
  transfers between devices with their start and end apart: 3, of which 3 were waited for; matrix products, arithmetic and copies ran while one was open for 0% of the time, Pallas kernels for 0%

commit v1 on v0

--- a/solution.py
+++ b/solution.py
@@ -45,7 +45,10 @@
 
 
 def local(psi, left_ops, right_ops, term_mask, pair_src, pair_dst):
-    whole = lax.all_gather(psi, "sec", axis=0, tiled=True)
+    size = lax.axis_size("sec")
+    shards = jnp.stack([psi for _ in range(size)])
+    shards = lax.all_to_all(shards, "sec", split_axis=0, concat_axis=0)
+    whole = jnp.concatenate(shards, axis=0)
     order = psi.shape[1]
     local_pairs = psi.shape[0]
     local_terms = left_ops.shape[1]

time: 218 us -> 351 us (1.61)
  waiting for transfers between devices: 115 us -> 236 us
  starting transfers between devices: 6.3 us -> 16.6 us
  local copies, waits for them, and re-layouts: 10.6 us -> 15.2 us
  loops' own time: 26.7 us -> 22.6 us
    all_to_all x0 -> x1, waiting for transfers between devices: none -> 182 us  [local(): shards = lax.all_to_all(shards, 'sec', split_axis=0, concat_axis=0)]
    all_gather x1 -> x0, waiting for transfers between devices: 60.7 us -> none  [local(): whole = lax.all_gather(psi, 'sec', axis=0, tiled=True)]
    all_to_all x0 -> x1, starting transfers between devices: none -> 9.97 us  [local(): shards = lax.all_to_all(shards, 'sec', split_axis=0, concat_axis=0)]
    another operation x0 -> x1, local copies, waits for them, and re-layouts: none -> 5.07 us  [local(): shards = jnp.stack([psi for _ in range(size)])]
where the time goes in v1:
time: 351 us; the launch traced here: 350 us
  waiting for transfers between devices  236 us (67%)
  loops' own time  22.6 us (6%)
  matrix products  21.6 us (6%)
  blocking collectives  17.1 us (5%)
  starting transfers between devices  16.6 us (5%)
  local copies, waits for them, and re-layouts  15.2 us (4%)
  between operations  14.9 us (4%)
  other arithmetic  5.37 us (2%)
    all_to_all x1, waiting for transfers between devices, local(): shards = lax.all_to_all(shards, 'sec', split_axis=0, concat_axis=0)  182 us
    all_gather x1, waiting for transfers between devices, in_one_piece(): lax.all_gather(both, axis, axis=dim, tiled=True)  38.9 us
    all_to_all x1, blocking collectives, copy_for_each(): lax.all_to_all(jnp.broadcast_to(value[None], (peers, *value.shape)), axis...  17.1 us
    all_to_all x1, waiting for transfers between devices, sent_and_summed(): lax.all_to_all(pieces, axis, split_axis=0, concat_axis=0, tiled=True)  15.5 us
    another operation x1, loops' own time, local(): lax.scan(term_step, (zero_block, zero_block), jnp.arange(local_terms, dty...  14 us
    all_to_all x1, starting transfers between devices, local(): shards = lax.all_to_all(shards, 'sec', split_axis=0, concat_axis=0)  9.97 us
    dot_general x5, matrix products, active(): jnp.dot(inner_adj, right, preferred_element_type=jnp.float32)  9.73 us
    dot_general x5, matrix products, active(): jnp.dot(inner_fwd, right.T, preferred_element_type=jnp.float32)  9.7 us
  transfers between devices with their start and end apart: 3, of which 3 were waited for; matrix products, arithmetic and copies ran while one was open for 0% of the time, Pallas kernels for 0%

profile of v1, /device:TPU:1, one launch (start us, length us, event | category | flops | bytes accessed | tf_op | source)
XLA Modules:
  0.0 349.9 jit_solution(2312460628661837069)
XLA Ops:
  6.5 5.1 %stack.8 = bf16[16,1,512,512]{3,2,1,0:T(8,128)(2,1)} broadcast(bf16[512,512]{1,0:T(8,128)(2,1)} %bitcast.71), dimensions={2,3} | broadcast | bytes 8912896 | tf_op jit(solution)/shard_map/stack | solution.py:49
  11.6 10.0 %all-to-all-start = ((bf16[16,1,512,512]{3,2,1,0:T(8,128)(2,1)}), bf16[16,1,512,512]{3,2,1,0:T(8,128)(2,1)}, u32[]{:S(2)}, u32[]{:S(2)}) async-start(bf16[16,1,512,512]{3,2,1,0:T(8,128)(2,1)} %stack.8), calls=%async_computation | async-start | bytes 16777216 | tf_op jit(solution)/shard_map/all_to_all | solution.py:50
  21.6 0.0 copy-start.1
  22.9 182.1 %all-to-all-done = bf16[16,1,512,512]{3,2,1,0:T(8,128)(2,1)} async-done(((bf16[16,1,512,512]{3,2,1,0:T(8,128)(2,1)}), bf16[16,1,512,512]{3,2,1,0:T(8,128)(2,1)}, u32[]{:S(2)}, u32[]{:S(2)}) %all-to-all-start) | async-done | bytes 8388640 | tf_op jit(solution)/shard_map/all_to_all | solution.py:50
  205.0 1.3 dynamic-slice_bitcast_fusion
  206.3 0.1 broadcast_in_dim.4
  206.4 0.1 broadcast_in_dim.4.clone
  206.5 0.0 copy-done.1
  206.5 49.3 %while.12 = (s32[]{:T(128)}, f32[512,512]{1,0:T(8,128)S(1)}, f32[512,512]{1,0:T(8,128)S(1)}, s32[6]{0:T(128)S(1)}, s32[1,6]{1,0:T(1,128)S(1)}, /*index=5*/bf16[1...) while((s32[]{:T(128)}, f32[512,512]{1,0:T(8,128)S(1)}, ...), condition=%wide.region_3.4_spmd, body=%wide.region_0.3_spmd.sunk | while | flops 1074790400 | bytes 7342387 | solution.py:79
  206.5 0.6 dynamic_slice.44
  208.8 0.6 fusion.29
  210.1 5.6 %conditional.2 = ((f32[512,512]{1,0:T(8,128)S(1)}, f32[512,512]{1,0:T(8,128)S(1)})) conditional(s32[]{:T(128)} %bitcast.56, (f32[512,512]{1,0:T(8,128)S(1)}, f32[512,512]{1,0:T(8,128)S(1)}) %tuple.30, (s32[]{:T(128)}, bf16[1,6,512,512]{3,2,1,0:T(8,128)(2,1)}, bf16[512,512]{1,0:T(8,128)(2,1)S(1)}, bf16[1,6,512,512]{3,2,1,0:T(8,128)(2,1)}, ...), branch_computations={%region_1.1_spmd, %region_2.2_spmd} | conditional | flops 1074790400 | bytes 7342138 | solution.py:77
  211.8 1.9 convolution_add_fusion
  213.7 1.9 convolution_add_fusion.1
  215.7 0.6 dynamic_slice.44
  217.9 0.6 fusion.29
  219.2 5.6 %conditional.2 = ((f32[512,512]{1,0:T(8,128)S(1)}, f32[512,512]{1,0:T(8,128)S(1)})) conditional(s32[]{:T(128)} %bitcast.56, (f32[512,512]{1,0:T(8,128)S(1)}, f32[512,512]{1,0:T(8,128)S(1)}) %tuple.30, (s32[]{:T(128)}, bf16[1,6,512,512]{3,2,1,0:T(8,128)(2,1)}, bf16[512,512]{1,0:T(8,128)(2,1)S(1)}, bf16[1,6,512,512]{3,2,1,0:T(8,128)(2,1)}, ...), branch_computations={%region_1.1_spmd, %region_2.2_spmd} | conditional | flops 1074790400 | bytes 7342138 | solution.py:77
  220.9 1.9 convolution_add_fusion
  222.9 1.9 convolution_add_fusion.1
  224.8 0.6 dynamic_slice.44
  227.1 0.6 fusion.29
  228.4 5.6 %conditional.2 = ((f32[512,512]{1,0:T(8,128)S(1)}, f32[512,512]{1,0:T(8,128)S(1)})) conditional(s32[]{:T(128)} %bitcast.56, (f32[512,512]{1,0:T(8,128)S(1)}, f32[512,512]{1,0:T(8,128)S(1)}) %tuple.30, (s32[]{:T(128)}, bf16[1,6,512,512]{3,2,1,0:T(8,128)(2,1)}, bf16[512,512]{1,0:T(8,128)(2,1)S(1)}, bf16[1,6,512,512]{3,2,1,0:T(8,128)(2,1)}, ...), branch_computations={%region_1.1_spmd, %region_2.2_spmd} | conditional | flops 1074790400 | bytes 7342138 | solution.py:77
  230.1 1.9 convolution_add_fusion
  232.0 1.9 convolution_add_fusion.1
  234.0 0.6 dynamic_slice.44
  236.2 0.6 fusion.29
  237.5 0.6 dynamic_slice.44
  239.8 0.6 fusion.29
  241.1 5.6 %conditional.2 = ((f32[512,512]{1,0:T(8,128)S(1)}, f32[512,512]{1,0:T(8,128)S(1)})) conditional(s32[]{:T(128)} %bitcast.56, (f32[512,512]{1,0:T(8,128)S(1)}, f32[512,512]{1,0:T(8,128)S(1)}) %tuple.30, (s32[]{:T(128)}, bf16[1,6,512,512]{3,2,1,0:T(8,128)(2,1)}, bf16[512,512]{1,0:T(8,128)(2,1)S(1)}, bf16[1,6,512,512]{3,2,1,0:T(8,128)(2,1)}, ...), branch_computations={%region_1.1_spmd, %region_2.2_spmd} | conditional | flops 1074790400 | bytes 7342138 | solution.py:77
  242.8 1.9 convolution_add_fusion
  244.7 1.9 convolution_add_fusion.1
  246.7 0.6 dynamic_slice.44
  249.0 0.6 fusion.29
  250.2 5.6 %conditional.2 = ((f32[512,512]{1,0:T(8,128)S(1)}, f32[512,512]{1,0:T(8,128)S(1)})) conditional(s32[]{:T(128)} %bitcast.56, (f32[512,512]{1,0:T(8,128)S(1)}, f32[512,512]{1,0:T(8,128)S(1)}) %tuple.30, (s32[]{:T(128)}, bf16[1,6,512,512]{3,2,1,0:T(8,128)(2,1)}, bf16[512,512]{1,0:T(8,128)(2,1)S(1)}, bf16[1,6,512,512]{3,2,1,0:T(8,128)(2,1)}, ...), branch_computations={%region_1.1_spmd, %region_2.2_spmd} | conditional | flops 1074790400 | bytes 7342138 | solution.py:77
  251.9 1.9 convolution_add_fusion
  253.9 1.9 convolution_add_fusion.1
  255.8 0.1 convert.10
  255.9 0.1 convert.9
  256.0 1.1 maximum_bitcast_fusion
  257.0 6.6 %all-to-all-start.1 = ((bf16[16,1,2,32,512]{4,3,2,1,0:T(8,128)(2,1)}), bf16[16,1,2,32,512]{4,3,2,1,0:T(8,128)(2,1)S(1)}, u32[]{:S(2)}, u32[]{:S(2)}) async-start(bf16[16,1,2,32,512]{4,3,2,1,0:T(8,128)(2,1)} %maximum_bitcast_fusion), calls=%async_computation.1 | async-start | bytes 2097152 | tf_op jit(solution)/shard_map/all_to_all | solution.py:15
  263.6 0.0 all-gather.3.cloned.1.call-start
  263.7 15.5 %all-to-all-done.1 = bf16[16,1,2,32,512]{4,3,2,1,0:T(8,128)(2,1)S(1)} async-done(((bf16[16,1,2,32,512]{4,3,2,1,0:T(8,128)(2,1)}), bf16[16,1,2,32,512]{4,3,2,1,0:T(8,128)(2,1)S(1)}, u32[]{:S(2)}, u32[]{:S(2)}) %all-to-all-start.1) | async-done | bytes 1048608 | tf_op jit(solution)/shard_map/all_to_all | solution.py:15
  279.2 0.1 convert_reduce_fusion
  279.3 0.1 reshape.94
  279.6 0.1 dynamic-update-slice.2
  279.7 0.0 copy-start
  279.7 0.7 copy-done
  280.4 0.0 all-gather.3.cloned.1.call-update
  280.4 38.9 %all-gather.3.cloned.1.call-done = f32[16,1,32770]{2,1,0:T(1,128)} async-done(((f32[1,1,32770]{2,1,0:T(1,128)}), f32[16,1,32770]{2,1,0:T(1,128)}) %all-gather.3.cloned.1.call-update) | async-done | bytes 2097296 | tf_op jit(solution)/shard_map/all_gather | solution.py:22
  319.3 1.7 copy.20
  321.0 0.1 slice.21
  321.2 1.2 copy.12
  322.4 0.3 slice_bitcast_fusion.1
  322.7 0.2 fusion.21
  322.8 1.1 fusion.18
  323.9 1.1 fusion.16
  325.1 17.1 %all_to_all.15 = bf16[16,1,32,512]{3,2,1,0:T(8,128)(2,1)S(1)} all-to-all(bf16[16,1,32,512]{3,2,1,0:T(8,128)(2,1)S(1)} %broadcast_in_dim.5), channel_id=1, replica_groups=mesh['sec'=16,'term'=16] {'term'}, dimensions={0} | all-to-all | bytes 1048576 | tf_op jit(solution)/shard_map/all_to_all | solution.py:38
  342.2 0.8 copy.39
  (6 shorter events, 0.1 us)
Async XLA Ops:
  11.6 193.4 %all-to-all-start = ((bf16[16,1,512,512]{3,2,1,0:T(8,128)(2,1)}), bf16[16,1,512,512]{3,2,1,0:T(8,128)(2,1)}, u32[]{:S(2)}, u32[]{:S(2)}) async-start(bf16[16,1,512,512]{3,2,1,0:T(8,128)(2,1)} %stack.8), calls=%async_computation | async-start | bytes 16777216 | tf_op jit(solution)/shard_map/all_to_all | solution.py:50
  21.6 184.9 %copy-start.1 = (s32[1,6]{1,0:T(1,128)S(1)}, s32[1,6]{1,0:T(1,128)}, u32[]{:S(2)}) copy-start(s32[1,6]{1,0:T(1,128)} %param.13) | copy-start | bytes 76
  257.0 22.1 %all-to-all-start.1 = ((bf16[16,1,2,32,512]{4,3,2,1,0:T(8,128)(2,1)}), bf16[16,1,2,32,512]{4,3,2,1,0:T(8,128)(2,1)S(1)}, u32[]{:S(2)}, u32[]{:S(2)}) async-start(bf16[16,1,2,32,512]{4,3,2,1,0:T(8,128)(2,1)} %maximum_bitcast_fusion), calls=%async_computation.1 | async-start | bytes 2097152 | tf_op jit(solution)/shard_map/all_to_all | solution.py:15
  263.6 55.6 %all-gather.3.cloned.1.call-start = ((), (), s32[]{:S(2)}) async-start(), calls=%async_computation.3 | async-start | bytes 2236928 | tf_op jit(solution)/shard_map/all_gather | solution.py:22
  279.7 0.7 copy-start
Sparse Core Ops, SparseCore 0:
  280.5 38.7 all-gather.2
